TPU v7x, 128 devices: a whole 4x4x4 slice. The times are simulated.
128 devices in a mesh: fsdp: 8 (over x, core), tensor: 2 (over y_lo), context: 8 (over z, y_hi).
Axes of the slice: x: 4, y: 4 (y_hi: 2, y_lo: 2; y = y_hi * 2 + y_lo), z: 4, core: 2. Of those that a mesh axis runs over, the one named last changes fastest.
Arguments:
- block_input: bfloat16 [16384, 768], P(('fsdp', 'context')), may hold values from -6 to 6
- seq_lengths: int32 [8, 3], P('fsdp'), may hold values from 1 to 1536, 2048 in all within a row
- attn_gain: bfloat16 [768], P('fsdp'), may hold values from 0.5 to 1.5
- qkv_weight: bfloat16 [768, 3, 768], P('fsdp', None, 'tensor'), may hold values from -0.3969283 to 0.3969283
- proj_weight: bfloat16 [768, 768], P('tensor', 'fsdp'), may hold values from -4 to 4
- mlp_gain: bfloat16 [768], P('fsdp'), may hold values from 0.5 to 1.5
- gelu_weight: bfloat16 [768, 2, 1152], P('fsdp', None, 'tensor'), may hold values from -0.21875 to 0.21875
- down_weight: bfloat16 [1152, 768], P('tensor', 'fsdp'), may hold values from -0.1875 to 0.1875
- out_cotangent: bfloat16 [16384, 768], P(('fsdp', 'context')), may hold values from -6 to 6
Outputs:
- block_output: bfloat16 [16384, 768], P(('fsdp', 'context'))
- input_grad: float32 [16384, 768], P(('fsdp', 'context'))
- attngain_grad: float32 [768], P('fsdp')
- qkv_grad: float32 [768, 3, 768], P('fsdp', None, 'tensor')
- proj_grad: float32 [768, 768], P('tensor', 'fsdp')
- mlpgain_grad: float32 [768], P('fsdp')
- gelu_grad: float32 [768, 2, 1152], P('fsdp', None, 'tensor')
- down_grad: float32 [1152, 768], P('tensor', 'fsdp')
All inputs are finite; a program needn't handle non-finite values.
Results may differ from a plain program's by a relative error of at most 0.02.
Values may be sent and summed in bfloat16 or wider, within the bound.
A program may use at most 128 MiB of HBM per device.

v0:
```python
import jax
import jax.numpy as jnp
from jax import lax
from jax.sharding import PartitionSpec as P

HD = 64
EPSILON = 1e-05
THETA = 160000.0
MASKED_LOW = -1e30


def layer_norm(values):
    centre = values - jnp.mean(values, axis=-1, keepdims=True)
    spread = lax.rsqrt(jnp.mean(centre * centre, axis=-1, keepdims=True) + EPSILON)
    return (centre * spread, spread)


def norm_back(grad_out, normed, spread, gain):
    scaled = grad_out * gain
    inner = jnp.mean(scaled, axis=-1, keepdims=True) + normed * jnp.mean(
        scaled * normed, axis=-1, keepdims=True
    )
    return spread * (scaled - inner)


def segments_of(row_ids, lengths):
    ends = jnp.cumsum(lengths)
    segment = jnp.sum((row_ids[:, None] >= ends[None, :]).astype(jnp.int32), axis=1)
    starts = ends - lengths
    picked = segment[:, None] == jnp.arange(lengths.shape[0], dtype=jnp.int32)[None, :]
    begin = jnp.sum(jnp.where(picked, starts[None, :], 0), axis=1)
    return (segment, row_ids - begin)


def rope_tables(positions, head_dim):
    half_dim = head_dim // 2
    exponent = jnp.arange(half_dim, dtype=jnp.float32) * (-2.0 / head_dim)
    frequency = jnp.power(jnp.float32(THETA), exponent)
    angles = positions.astype(jnp.float32)[:, None] * frequency[None, :]
    return (jnp.cos(angles)[:, None, :], jnp.sin(angles)[:, None, :])


def rotate(values, cosine, sine_tab):
    half_dim = values.shape[-1] // 2
    lower_half, upper_half = (values[..., :half_dim], values[..., half_dim:])
    return jnp.concatenate(
        [lower_half * cosine - upper_half * sine_tab, upper_half * cosine + lower_half * sine_tab],
        axis=-1,
    )


def rotate_back(grads, cosine, sine_tab):
    half_dim = grads.shape[-1] // 2
    lower_half, upper_half = (grads[..., :half_dim], grads[..., half_dim:])
    return jnp.concatenate(
        [lower_half * cosine + upper_half * sine_tab, upper_half * cosine - lower_half * sine_tab],
        axis=-1,
    )


def gelu_parts(gate_pre):
    normal_cdf = 0.5 * (1.0 + jax.scipy.special.erf(gate_pre * 0.7071067811865476))
    density = jnp.exp(-0.5 * gate_pre * gate_pre) * 0.3989422804014327
    return (gate_pre * normal_cdf, normal_cdf + gate_pre * density)


def split_count(row_count):
    pieces = 1
    while row_count // pieces > 1024 and row_count % (2 * pieces) == 0:
        pieces = pieces * 2
    return pieces


def over_blocks(step, running, members):
    row_count = members[0].shape[0]
    pieces = split_count(row_count)
    stride = row_count // pieces

    def one_block(counter, current):
        offset = counter * stride
        sliced = tuple((lax.dynamic_slice_in_dim(member, offset, stride, 0) for member in members))
        return step(current, sliced, offset)

    return lax.fori_loop(0, pieces, one_block, running)


def guarded(step):

    def wrapped(running, members, first_row):
        return step(running, members, first_row)

    def folded(running, members, first_row):
        return over_blocks(wrapped, running, members)

    return folded


def on_device(
    block_input,
    seq_lengths,
    attn_gain,
    qkv_weight,
    proj_weight,
    mlp_gain,
    gelu_weight,
    down_weight,
    out_cotangent,
):
    row_count = block_input.shape[0]
    feature_count = block_input.shape[1]
    lengths = seq_lengths[0]
    group_rows = row_count * lax.axis_size("context")
    own_first = lax.axis_index("context") * row_count
    own_rows = own_first + jnp.arange(row_count, dtype=jnp.int32)
    own_segment, positions = segments_of(own_rows, lengths)
    cosine, sine_tab = rope_tables(positions, HD)
    gathered = (
        lax.all_gather(qkv_weight, "fsdp", axis=0, tiled=True),
        lax.all_gather(proj_weight, "fsdp", axis=1, tiled=True),
        lax.all_gather(gelu_weight, "fsdp", axis=0, tiled=True),
        lax.all_gather(down_weight, "fsdp", axis=1, tiled=True),
        lax.all_gather(attn_gain, "fsdp", axis=0, tiled=True),
        lax.all_gather(mlp_gain, "fsdp", axis=0, tiled=True),
    )
    qkv_full, proj_full, gelu_full, down_full, attn_full, mlp_full = gathered
    local_width = qkv_full.shape[2]
    head_count = local_width // HD
    hidden = gelu_full.shape[2]
    attn_scale = attn_full.astype(jnp.float32)
    mlp_scale = mlp_full.astype(jnp.float32)
    inputs = block_input.astype(jnp.float32)
    normed_attn, spread_attn = layer_norm(inputs)
    hidden_attn = (normed_attn * attn_scale).astype(jnp.bfloat16)
    qkv_flat = qkv_full.reshape(feature_count, 3 * local_width)
    projected = jnp.dot(hidden_attn, qkv_flat, preferred_element_type=jnp.float32).reshape(
        row_count, 3, head_count, HD
    )
    query_bf = rotate(projected[:, 0], cosine, sine_tab).astype(jnp.bfloat16)
    key_bf = rotate(projected[:, 1], cosine, sine_tab).astype(jnp.bfloat16)
    value_bf = projected[:, 2].astype(jnp.bfloat16)
    key_flat = key_bf.reshape(row_count, local_width)
    value_flat = value_bf.reshape(row_count, local_width)
    keys_group, values_group = (
        lax.all_gather(key_flat, "context", axis=0, tiled=True),
        lax.all_gather(value_flat, "context", axis=0, tiled=True),
    )
    keys_heads = keys_group.reshape(group_rows, head_count, HD)
    values_heads = values_group.reshape(group_rows, head_count, HD)
    group_segment, unused_pos = segments_of(jnp.arange(group_rows, dtype=jnp.int32), lengths)
    same_group = (own_segment[:, None] == group_segment[None, :])[None]
    fwd_scores = (
        jnp.einsum("qhd,khd->hqk", query_bf, keys_heads, preferred_element_type=jnp.float32) * 0.125
    )
    row_max = jnp.max(jnp.where(same_group, fwd_scores, MASKED_LOW), axis=2)
    denom_sum = jnp.sum(
        jnp.where(same_group, jnp.exp(fwd_scores - row_max[:, :, None]), 0.0), axis=2
    )
    log_total = row_max + jnp.log(denom_sum)
    fwd_weights = jnp.where(same_group, jnp.exp(fwd_scores - log_total[:, :, None]), 0.0).astype(
        jnp.bfloat16
    )
    mixed = jnp.einsum(
        "hqk,khd->qhd", fwd_weights, values_heads, preferred_element_type=jnp.float32
    ).astype(jnp.bfloat16)
    mixed_flat = mixed.reshape(row_count, local_width)
    attn_part = jnp.dot(mixed_flat, proj_full, preferred_element_type=jnp.float32)
    residual = inputs + lax.psum(attn_part, "tensor")
    normed_mlp, spread_mlp = layer_norm(residual)
    hidden_mlp = (normed_mlp * mlp_scale).astype(jnp.bfloat16)
    gelu_flat = gelu_full.reshape(feature_count, 2 * hidden)
    gate_up = jnp.dot(hidden_mlp, gelu_flat, preferred_element_type=jnp.float32).reshape(
        row_count, 2, hidden
    )
    gate_pre, up_pre = (gate_up[:, 0], gate_up[:, 1])
    gelu_val, gelu_slope = gelu_parts(gate_pre)
    activ = (gelu_val * up_pre).astype(jnp.bfloat16)
    mlp_part = jnp.dot(activ, down_full, preferred_element_type=jnp.float32)
    block_output = (
        residual + lax.psum(mlp_part.astype(jnp.bfloat16), "tensor").astype(jnp.float32)
    ).astype(jnp.bfloat16)
    act_grad = jnp.dot(out_cotangent, down_full.T, preferred_element_type=jnp.float32)
    down_grad_t = jnp.dot(out_cotangent.T, activ, preferred_element_type=jnp.float32)
    gate_up_grad = (
        jnp.stack([act_grad * up_pre * gelu_slope, act_grad * gelu_val], axis=1)
        .astype(jnp.bfloat16)
        .reshape(row_count, 2 * hidden)
    )
    gelu_grad = jnp.dot(hidden_mlp.T, gate_up_grad, preferred_element_type=jnp.float32).reshape(
        feature_count, 2, hidden
    )
    mlp_in_grad = lax.psum(
        jnp.dot(gate_up_grad, gelu_flat.T, preferred_element_type=jnp.float32), "tensor"
    )
    mlpgain_grad = jnp.sum(mlp_in_grad * normed_mlp, axis=0)
    resid_grad = out_cotangent.astype(jnp.float32) + norm_back(
        mlp_in_grad, normed_mlp, spread_mlp, mlp_scale
    )
    resid_bf = resid_grad.astype(jnp.bfloat16)
    out_grad = jnp.dot(resid_bf, proj_full.T, preferred_element_type=jnp.float32).astype(
        jnp.bfloat16
    )
    proj_grad_t = jnp.dot(resid_bf.T, mixed_flat, preferred_element_type=jnp.float32)
    out_heads = out_grad.reshape(row_count, head_count, HD)
    delta = jnp.transpose(
        jnp.sum(out_heads.astype(jnp.float32) * mixed.astype(jnp.float32), axis=2)
    )

    def key_terms(members, first_row):
        key_count = members[0].shape[0]
        key_part = members[0].reshape(key_count, head_count, HD)
        value_part = members[1].reshape(key_count, head_count, HD)
        key_segment, unused = segments_of(
            first_row + jnp.arange(key_count, dtype=jnp.int32), lengths
        )
        same_doc = (own_segment[:, None] == key_segment[None, :])[None]
        scores = (
            jnp.einsum("qhd,khd->hqk", query_bf, key_part, preferred_element_type=jnp.float32)
            * 0.125
        )
        weights = jnp.where(same_doc, jnp.exp(scores - log_total[:, :, None]), 0.0)
        prob_grad = jnp.einsum(
            "qhd,khd->hqk", out_heads, value_part, preferred_element_type=jnp.float32
        )
        score_grad = (weights * (prob_grad - delta[:, :, None])).astype(jnp.bfloat16)
        return (key_part, weights, score_grad)

    def owner_step(running, members, first_row):
        query_grad, key_all, value_all = running
        key_part, weights, score_grad = key_terms(members, first_row)
        key_count = key_part.shape[0]
        query_grad = (
            query_grad
            + jnp.einsum("hqk,khd->qhd", score_grad, key_part, preferred_element_type=jnp.float32)
            * 0.125
        )
        key_piece = (
            jnp.einsum(
                "hqk,qhd->khd", score_grad, query_bf, preferred_element_type=jnp.float32
            ).reshape(key_count, local_width)
            * 0.125
        )
        value_piece = jnp.einsum(
            "hqk,qhd->khd",
            weights.astype(jnp.bfloat16),
            out_heads,
            preferred_element_type=jnp.float32,
        ).reshape(key_count, local_width)
        key_all = lax.dynamic_update_slice_in_dim(
            key_all,
            lax.dynamic_slice_in_dim(key_all, first_row, key_count, 0) + key_piece,
            first_row,
            0,
        )
        value_all = lax.dynamic_update_slice_in_dim(
            value_all,
            lax.dynamic_slice_in_dim(value_all, first_row, key_count, 0) + value_piece,
            first_row,
            0,
        )
        return (query_grad, key_all, value_all)

    grad_start = jnp.zeros((row_count, head_count, HD), jnp.float32)
    back_state = (
        grad_start,
        jnp.zeros((group_rows, local_width), jnp.float32),
        jnp.zeros((group_rows, local_width), jnp.float32),
    )
    back_result = guarded(owner_step)(
        back_state,
        (
            lax.all_gather(key_flat, "context", axis=0, tiled=True),
            lax.all_gather(value_flat, "context", axis=0, tiled=True),
        ),
        jnp.int32(0),
    )
    query_grad = back_result[0]
    key_grad, value_grad = (
        lax.psum_scatter(
            back_result[1].astype(jnp.bfloat16), "context", scatter_dimension=0, tiled=True
        ).astype(jnp.float32),
        lax.psum_scatter(
            back_result[2].astype(jnp.bfloat16), "context", scatter_dimension=0, tiled=True
        ).astype(jnp.float32),
    )
    key_grad = key_grad.reshape(row_count, head_count, HD)
    value_grad = value_grad.reshape(row_count, head_count, HD)
    qkv_rows = (
        jnp.stack(
            [
                rotate_back(query_grad, cosine, sine_tab),
                rotate_back(key_grad, cosine, sine_tab),
                value_grad,
            ],
            axis=1,
        )
        .astype(jnp.bfloat16)
        .reshape(row_count, 3 * local_width)
    )
    qkv_grad = jnp.dot(hidden_attn.T, qkv_rows, preferred_element_type=jnp.float32).reshape(
        feature_count, 3, local_width
    )
    attn_in_grad = lax.psum(
        jnp.dot(qkv_rows, qkv_flat.T, preferred_element_type=jnp.float32).astype(jnp.bfloat16),
        "tensor",
    ).astype(jnp.float32)
    attngain_grad = jnp.sum(attn_in_grad * normed_attn, axis=0)
    input_grad = resid_grad + norm_back(attn_in_grad, normed_attn, spread_attn, attn_scale)
    grads = (
        attngain_grad[:, None],
        mlpgain_grad[:, None],
        qkv_grad.reshape(feature_count, 3 * local_width),
        gelu_grad.reshape(feature_count, 2 * hidden),
        proj_grad_t,
        down_grad_t,
    )
    widths = [g.shape[1] for g in grads]
    packed = jnp.concatenate(grads, axis=1)
    packed = lax.psum_scatter(packed, "fsdp", scatter_dimension=0, tiled=True)
    packed = lax.psum(packed, "context")
    pieces = []
    start = 0
    for width in widths:
        pieces.append(packed[:, start : start + width])
        start += width
    shard_rows = packed.shape[0]
    shares = (
        pieces[0][:, 0],
        pieces[2].reshape(shard_rows, 3, local_width),
        pieces[4].T,
        pieces[1][:, 0],
        pieces[3].reshape(shard_rows, 2, hidden),
        pieces[5].T,
    )
    return (
        block_output,
        input_grad,
        shares[0],
        shares[1],
        shares[2],
        shares[3],
        shares[4],
        shares[5],
    )


def solution(mesh):
    in_specs = (
        P(("fsdp", "context"), None),
        P("fsdp", None),
        P("fsdp"),
        P("fsdp", None, "tensor"),
        P("tensor", "fsdp"),
        P("fsdp"),
        P("fsdp", None, "tensor"),
        P("tensor", "fsdp"),
        P(("fsdp", "context"), None),
    )
    out_specs = (
        P(("fsdp", "context"), None),
        P(("fsdp", "context"), None),
        P("fsdp"),
        P("fsdp", None, "tensor"),
        P("tensor", "fsdp"),
        P("fsdp"),
        P("fsdp", None, "tensor"),
        P("tensor", "fsdp"),
    )
    return jax.shard_map(
        on_device, mesh=mesh, in_specs=in_specs, out_specs=out_specs, check_vma=False
    )
```

profile of v0, /device:TPU:0, one launch (start us, length us, event | category | flops | bytes accessed | tf_op | source)
XLA Modules:
  0.0 698.4 jit_solution(5407401806397029626)
XLA Ops:
  11.6 14.7 %all-reduce.2 = (bf16[768]{0:T(1024)(128)(2,1)S(1)}, bf16[768]{0:T(1024)(128)(2,1)S(1)}) all-reduce(bf16[768]{0:T(1024)(128)(2,1)S(1)} %dynamic-update-slice, bf16[768]{0:T(1024)(128)(2,1)S(1)} %dynamic-update-slice.1), channel_id=1, replica_groups=mesh['fsdp'=8,'tensor'=2,'context'=8] {'fsdp'}, use_global_device_ids=true, to_apply=%add | all-reduce | flops 1536 | bytes 6144
  30.6 6.5 all-gather.5.cloned.1.call-done
  37.1 2.6 copy.52
  45.6 13.2 %all_gather.30 = bf16[384,768]{0,1:T(8,128)(2,1)S(1)} all-gather(bf16[384,96]{0,1:T(8,128)(2,1)S(1)} %copy-done.46), channel_id=1, replica_groups=mesh['fsdp'=8,'tensor'=2,'context'=8] {'fsdp'}, dimensions={1}, use_global_device_ids=true | all-gather | bytes 663552 | tf_op jit(solution)/shard_map/all_gather | solution.py:119
  58.8 33.9 %all-gather.9.cloned.1.call-done = bf16[2048,384]{0,1:T(8,128)(2,1)} async-done(((bf16[256,384]{0,1:T(8,128)(2,1)}), bf16[2048,384]{0,1:T(8,128)(2,1)}) %all-gather.9.cloned.1.call-update) | async-done | bytes 1572880 | tf_op jit(solution)/shard_map/all_gather | solution.py:144
  92.7 3.9 select_reduce_fusion.1
  96.6 3.9 select_reduce_fusion
  101.1 42.2 %all-gather.7.cloned.1.call-done = bf16[2048,384]{0,1:T(8,128)(2,1)} async-done(((bf16[256,384]{0,1:T(8,128)(2,1)}), bf16[2048,384]{0,1:T(8,128)(2,1)}) %all-gather.7.cloned.1.call-update) | async-done | bytes 1572880 | tf_op jit(solution)/shard_map/all_gather | solution.py:145
  143.3 7.7 %fusion.13 = bf16[6,64,256]{2,1,0:T(8,128)(2,1)S(1)} fusion(bf16[2048,6,64]{0,2,1:T(8,128)(2,1)} %bitcast.184, f32[6,256,2048]{2,1,0:T(8,128)} %copy-done.7, f32[6,256]{1,0:T(8,128)S(1)} %log_add_fusion, pred[256,2048]{1,0:T(8,128)(4,1)S(1)} %broadcast_compare_fusion.1), kind=kOutput, calls=%fused_computation.37 | convolution fusion | flops 415334400 | bytes 14882816 | tf_op jit(solution)/shard_map/hqk,khd->qhd/dot_general | solution.py:162
  152.4 16.8 %all_gather.33 = bf16[576,768]{0,1:T(8,128)(2,1)} all-gather(bf16[576,96]{0,1:T(8,128)(2,1)S(1)} %copy-done.45), channel_id=1, replica_groups=mesh['fsdp'=8,'tensor'=2,'context'=8] {'fsdp'}, dimensions={1}, use_global_device_ids=true | all-gather | bytes 995328 | tf_op jit(solution)/shard_map/all_gather | solution.py:121
  170.0 2.7 copy.54
  172.7 40.8 %all-reduce.9.cloned.1.call-done = f32[256,768]{1,0:T(8,128)} async-done(((f32[256,768]{1,0:T(8,128)}), f32[256,768]{1,0:T(8,128)}) %all-reduce.9.cloned.1.call-update) | async-done | bytes 786448 | tf_op jit(solution)/shard_map/psum | solution.py:167
  219.8 41.8 %all-reduce.11.cloned.1.call-done = f32[256,768]{1,0:T(8,128)} async-done(((f32[256,768]{1,0:T(8,128)}), f32[256,768]{1,0:T(8,128)}) %all-reduce.11.cloned.1.call-update) | async-done | bytes 786448 | tf_op jit(solution)/shard_map/psum | solution.py:191
  261.6 2.1 multiply_reduce_fusion
  266.4 2.1 broadcast.210
  270.5 40.4 %while.20 = (s32[]{:T(128)}, f32[256,6,64]{0,2,1:T(8,128)}, f32[2048,384]{0,1:T(8,128)}, f32[2048,384]{0,1:T(8,128)}, bf16[2048,384]{0,1:T(8,128)(2,1)}, /*index...) while((s32[]{:T(128)}, f32[256,6,64]{0,2,1:T(8,128)}, ...), condition=%wide.region_19.20_spmd.clone, body=%wide.region_17.19_spmd.clone.sunk | while | flops 1024107520 | bytes 131182336 | solution.py:84
  275.0 3.3 fusion.105
  278.4 2.6 fusion.106
  281.0 4.3 fusion.107
  295.2 3.3 fusion.105
  298.6 2.7 fusion.106
  301.2 4.3 fusion.107
  310.9 3.4 convert_element_type.160
  318.9 2.7 fusion.48
  321.6 67.5 %reduce-scatter.4.cloned.1.call-done = bf16[256,384]{0,1:T(8,128)(2,1)} async-done(((bf16[2048,384]{0,1:T(8,128)(2,1)}), bf16[256,384]{0,1:T(8,128)(2,1)}) %reduce-scatter.4.cloned.1.call-update) | async-done | bytes 196624 | tf_op jit(solution)/shard_map/reduce_scatter | solution.py:278
  391.1 74.7 %reduce-scatter.6.cloned.1.call-done = bf16[256,384]{0,1:T(8,128)(2,1)} async-done(((bf16[2048,384]{0,1:T(8,128)(2,1)}), bf16[256,384]{0,1:T(8,128)(2,1)}) %reduce-scatter.6.cloned.1.call-update) | async-done | bytes 196624 | tf_op jit(solution)/shard_map/reduce_scatter | solution.py:281
  469.1 3.0 convolution_bitcast_fusion
  473.7 2.6 fusion.45
  476.3 32.8 %all-reduce.15.cloned.1.call-done = (bf16[256,768]{1,0:T(8,128)(2,1)}, bf16[256,768]{1,0:T(8,128)(2,1)}) async-done(((bf16[256,768]{1,0:T(8,128)(2,1)}, bf16[256,768]{1,0:T(8,128)(2,1)}), (bf16[256,768]{1,0:T(8,128)(2,1)}, bf16[256,768]{1,0:T(8,128)(2,1)})) %all-reduce.15.cloned.1.call-update) | async-done | bytes 786448 | tf_op jit(solution)/shard_map/psum | solution.py:179
  510.7 13.5 %concatenate.21 = f32[768,3266]{1,0:T(8,128)} concatenate(f32[768,1]{1,0:T(8,128)S(1)} %broadcast_in_dim.141, f32[768,1]{1,0:T(8,128)S(1)} %broadcast_in_dim.142, f32[768,1152]{1,0:T(8,128)} %fusion.45, f32[768,1152]{1,0:T(8,128)} %fusion.48, f32[768,384]{1,0:T(8,128)} %fusion.38, f32[768,576]{1,0:T(8,128)} %convolution_bitcast_fusion), dimensions={1} | concatenate | bytes 20066304 | tf_op jit(solution)/shard_map/concatenate | solution.py:317
  524.3 62.2 %reduce-scatter.8.cloned.1.call-done = f32[96,3266]{1,0:T(8,128)} async-done(((f32[768,3266]{1,0:T(8,128)}), f32[96,3266]{1,0:T(8,128)}) %reduce-scatter.8.cloned.1.call-update) | async-done | bytes 1254160 | tf_op jit(solution)/shard_map/reduce_scatter | solution.py:318
  588.6 94.9 %all-reduce.13.cloned.1.call-done = f32[96,3266]{1,0:T(8,128)} async-done(((f32[96,3266]{1,0:T(8,128)}), f32[96,3266]{1,0:T(8,128)}) %all-reduce.13.cloned.1.call-update) | async-done | bytes 1254160 | tf_op jit(solution)/shard_map/psum | solution.py:319
  (264 shorter events, 70.3 us)
Async XLA Ops:
  7.2 32.6 %copy-start.10 = (bf16[256,768]{1,0:T(8,128)(2,1)S(1)}, bf16[256,768]{1,0:T(8,128)(2,1)}, u32[]{:S(2)}) copy-start(bf16[256,768]{1,0:T(8,128)(2,1)} %param.11) | copy-start | bytes 1179652
  7.2 29.9 %all-gather.5.cloned.1.call-start = ((), (), s32[]{:S(2)}) async-start(), calls=%async_computation.3 | async-start | bytes 1990656 | tf_op jit(solution)/shard_map/all_gather | solution.py:118
  7.9 84.8 %all-gather.9.cloned.1.call-start = ((), (), s32[]{:S(2)}) async-start(), calls=%async_computation.5 | async-start | bytes 1769472 | tf_op jit(solution)/shard_map/all_gather | solution.py:144
  30.3 10.2 %copy-start.50 = (f32[256]{0:T(256)}, f32[256]{0:T(256)S(1)}, u32[]{:S(2)}) copy-start(f32[256]{0:T(256)S(1)} %add_rsqrt_fusion.1) | copy-start | bytes 3076
  30.6 11.1 %copy-start.40 = (f32[256,32]{0,1:T(8,128)}, f32[256,32]{0,1:T(8,128)S(1)}, u32[]{:S(2)}) copy-start(f32[256,32]{0,1:T(8,128)S(1)} %get-tuple-element.417) | copy-start | bytes 98308
  30.6 11.1 %copy-start.41 = (f32[256,32]{0,1:T(8,128)}, f32[256,32]{0,1:T(8,128)S(1)}, u32[]{:S(2)}) copy-start(f32[256,32]{0,1:T(8,128)S(1)} %get-tuple-element.418) | copy-start | bytes 98308
  41.8 54.8 %copy-start.33 = (bf16[256,6,32]{0,2,1:T(8,128)(2,1)}, bf16[256,6,32]{0,2,1:T(8,128)(2,1)S(1)}, u32[]{:S(2)}) copy-start(bf16[256,6,32]{0,2,1:T(8,128)(2,1)S(1)} %get-tuple-element.409) | copy-start | bytes 294916
  41.8 54.8 %copy-start.35 = (bf16[256,6,32]{0,2,1:T(8,128)(2,1)}, bf16[256,6,32]{0,2,1:T(8,128)(2,1)S(1)}, u32[]{:S(2)}) copy-start(bf16[256,6,32]{0,2,1:T(8,128)(2,1)S(1)} %get-tuple-element.410) | copy-start | bytes 294916
  42.5 100.8 %all-gather.7.cloned.1.call-start = ((), (), s32[]{:S(2)}) async-start(), calls=%async_computation.4 | async-start | bytes 1769472 | tf_op jit(solution)/shard_map/all_gather | solution.py:145
  44.3 125.7 %all-gather.11.cloned.1.call-start = ((), (), s32[]{:S(2)}) async-start(), calls=%async_computation.7 | async-start | bytes 2211840 | tf_op jit(solution)/shard_map/all_gather | solution.py:120
  45.1 168.4 %all-reduce.9.cloned.1.call-start = ((), (), s32[]{:S(2)}) async-start(), calls=%async_computation.6 | async-start | bytes 1572864 | tf_op jit(solution)/shard_map/psum | solution.py:167
  58.8 92.1 %copy-start.19 = (bf16[384,768]{0,1:T(8,128)(2,1)}, bf16[384,768]{0,1:T(8,128)(2,1)S(1)}, u32[]{:S(2)}) copy-start(bf16[384,768]{0,1:T(8,128)(2,1)S(1)} %all_gather.30) | copy-start | bytes 1769476
  101.1 49.8 %copy-start.58 = (f32[6,256]{1,0:T(8,128)}, f32[6,256]{1,0:T(8,128)S(1)}, u32[]{:S(2)}) copy-start(f32[6,256]{1,0:T(8,128)S(1)} %log_add_fusion) | copy-start | bytes 18436
  143.3 9.1 %copy-start.45 = (bf16[576,96]{0,1:T(8,128)(2,1)S(1)}, bf16[576,96]{0,1:T(8,128)(2,1)}, u32[]{:S(2)}) copy-start(bf16[576,96]{0,1:T(8,128)(2,1)} %param.18) | copy-start | bytes 331780
  152.3 109.3 %all-reduce.11.cloned.1.call-start = ((), (), s32[]{:S(2)}) async-start(), calls=%async_computation.8 | async-start | bytes 1572864 | tf_op jit(solution)/shard_map/psum | solution.py:191
  172.7 44.1 %copy-start.31 = (bf16[256,768]{1,0:T(8,128)(2,1)S(1)}, bf16[256,768]{1,0:T(8,128)(2,1)}, u32[]{:S(2)}) copy-start(bf16[256,768]{1,0:T(8,128)(2,1)} %param.19) | copy-start | bytes 1179652
  214.9 48.9 %copy-start.8 = (f32[256,768]{1,0:T(8,128)}, f32[256,768]{1,0:T(8,128)S(1)}, u32[]{:S(2)}) copy-start(f32[256,768]{1,0:T(8,128)S(1)} %get-tuple-element.396) | copy-start | bytes 2359300
  217.5 46.2 %copy-start.42 = (bf16[256,1,576]{0,2,1:T(8,128)(2,1)}, bf16[256,1,576]{0,2,1:T(8,128)(2,1)S(1)}, u32[]{:S(2)}) copy-start(bf16[256,1,576]{0,2,1:T(8,128)(2,1)S(1)} %get-tuple-element.399) | copy-start | bytes 884740
  217.5 46.2 %copy-start.43 = (bf16[256,1,576]{0,2,1:T(8,128)(2,1)}, bf16[256,1,576]{0,2,1:T(8,128)(2,1)S(1)}, u32[]{:S(2)}) copy-start(bf16[256,1,576]{0,2,1:T(8,128)(2,1)S(1)} %get-tuple-element.400) | copy-start | bytes 884740
  217.5 44.1 %copy-start.48 = (f32[256]{0:T(256)S(1)}, f32[256]{0:T(256)}, u32[]{:S(2)}) copy-start(f32[256]{0:T(256)} %copy-done.47) | copy-start | bytes 3076
  217.5 44.1 %copy-start.53 = (f32[256]{0:T(256)S(1)}, f32[256]{0:T(256)}, u32[]{:S(2)}) copy-start(f32[256]{0:T(256)} %copy-done.52) | copy-start | bytes 3076
  217.8 45.9 %copy-start.32 = (bf16[256,768]{1,0:T(8,128)(2,1)S(1)}, bf16[256,768]{1,0:T(8,128)(2,1)}, u32[]{:S(2)}) copy-start(bf16[256,768]{1,0:T(8,128)(2,1)} %param.19) | copy-start | bytes 1179652
  219.6 45.6 %copy-start.20 = (bf16[384,768]{0,1:T(8,128)(2,1)S(1)}, bf16[384,768]{0,1:T(8,128)(2,1)}, u32[]{:S(2)}) copy-start(bf16[384,768]{0,1:T(8,128)(2,1)} %copy-done.19) | copy-start | bytes 1769476
  219.6 169.6 %reduce-scatter.4.cloned.1.call-start = ((), (), s32[]{:S(2)}) async-start(), calls=%async_computation.9 | async-start | bytes 1769472 | tf_op jit(solution)/shard_map/reduce_scatter | solution.py:278
  314.4 151.4 %reduce-scatter.6.cloned.1.call-start = ((), (), s32[]{:S(2)}) async-start(), calls=%async_computation.10 | async-start | bytes 1769472 | tf_op jit(solution)/shard_map/reduce_scatter | solution.py:281
  315.9 193.2 %all-reduce.15.cloned.1.call-start = ((), (), s32[]{:S(2)}) async-start(), calls=%async_computation.13 | async-start | bytes 1572864 | tf_op jit(solution)/shard_map/psum | solution.py:179
  318.9 71.2 %copy-start.14 = (f32[256,6,64]{0,2,1:T(8,128)S(1)}, f32[256,6,64]{0,2,1:T(8,128)}, u32[]{:S(2)}) copy-start(f32[256,6,64]{0,2,1:T(8,128)} %get-tuple-element.285) | copy-start | bytes 1179652
  318.9 148.7 %copy-start.13 = (bf16[768,3,384]{0,2,1:T(8,128)(2,1)S(1)}, bf16[768,3,384]{0,2,1:T(8,128)(2,1)}, u32[]{:S(2)}) copy-start(bf16[768,3,384]{0,2,1:T(8,128)(2,1)} %copy-done.12) | copy-start | bytes 5308420
  469.1 117.4 %reduce-scatter.8.cloned.1.call-start = ((), (), s32[]{:S(2)}) async-start(), calls=%async_computation.11 | async-start | bytes 11501568 | tf_op jit(solution)/shard_map/reduce_scatter | solution.py:318
  524.2 62.3 %copy-start.39 = (bf16[256,768]{1,0:T(8,128)(2,1)S(1)}, bf16[256,768]{1,0:T(8,128)(2,1)}, u32[]{:S(2)}) copy-start(bf16[256,768]{1,0:T(8,128)(2,1)} %get-tuple-element.393) | copy-start | bytes 1179652
  524.2 63.2 %copy-start.30 = (bf16[256,768]{1,0:T(8,128)(2,1)S(1)}, bf16[256,768]{1,0:T(8,128)(2,1)}, u32[]{:S(2)}) copy-start(bf16[256,768]{1,0:T(8,128)(2,1)} %get-tuple-element.394) | copy-start | bytes 1179652
  524.3 159.2 %all-reduce.13.cloned.1.call-start = ((), (), s32[]{:S(2)}) async-start(), calls=%async_computation.12 | async-start | bytes 2555904 | tf_op jit(solution)/shard_map/psum | solution.py:319
  (57 other events, 174.0 us)
Sparse Core Ops, SparseCore 0:
  9.7 27.3 all-gather.4
  42.7 50.0 all-gather.8
  95.5 47.7 all-gather.6
  145.4 24.5 all-gather.10
  172.8 40.5 all-reduce.8
  219.7 41.8 all-reduce.10
  314.5 74.6 reduce-scatter.3
  393.3 72.4 reduce-scatter.5
  469.2 39.8 all-reduce.14
  524.4 62.0 reduce-scatter.7
  589.2 94.2 all-reduce.12
where the time goes:
time: 700 us; the launch traced here: 698 us
  waiting for transfers between devices  499 us (71%)
  matrix products  54.2 us (8%)
  local copies, waits for them, and re-layouts  54.1 us (8%)
  blocking collectives  44.7 us (6%)
  other arithmetic  30.3 us (4%)
  between operations  15.2 us (2%)
    psum x1, waiting for transfers between devices, on_device(): packed = lax.psum(packed, 'context')  94.9 us
    reduce_scatter x1, waiting for transfers between devices, on_device(): lax.psum_scatter(back_result[2].astype(jnp.bfloat16), 'context', scatter_...  74.7 us
    reduce_scatter x1, waiting for transfers between devices, on_device(): lax.psum_scatter(back_result[1].astype(jnp.bfloat16), 'context', scatter_...  67.5 us
    reduce_scatter x1, waiting for transfers between devices, on_device(): packed = lax.psum_scatter(packed, 'fsdp', scatter_dimension=0, tiled=True)  62.2 us
    all_gather x1, waiting for transfers between devices, on_device(): lax.all_gather(value_flat, 'context', axis=0, tiled=True)  42.2 us
    psum x1, waiting for transfers between devices, on_device(): lax.psum(jnp.dot(gate_up_grad, gelu_flat.T, preferred_element_type=jnp.fl...  41.8 us
    psum x1, waiting for transfers between devices, on_device(): residual = inputs + lax.psum(attn_part, 'tensor')  40.8 us
    all_gather x1, waiting for transfers between devices, on_device(): lax.all_gather(key_flat, 'context', axis=0, tiled=True)  33.9 us
  transfers between devices with their start and end apart: 11, of which 11 were waited for; matrix products, arithmetic and copies ran while one was open for 7% of the time, Pallas kernels for 0%

commit v1 on v0

--- a/solution.py
+++ b/solution.py
@@ -114,11 +114,48 @@
     own_rows = own_first + jnp.arange(row_count, dtype=jnp.int32)
     own_segment, positions = segments_of(own_rows, lengths)
     cosine, sine_tab = rope_tables(positions, HD)
+
+    def mark_the_body(packet, device_axis, dim_at):
+        seen_now, x_next, new = (
+            lax.axis_size(device_axis),
+            lax.axis_index(device_axis),
+            packet.shape[dim_at],
+        )
+        front = lax.dynamic_update_slice_in_dim(
+            jnp.zeros(
+                tuple((s * seen_now if nth == dim_at else s for nth, s in enumerate(packet.shape))),
+                packet.dtype,
+            ),
+            packet,
+            x_next * new,
+            axis=dim_at,
+        )
+        all_values = x_new = packet
+        for w in range(1, seen_now // 2 + 1):
+            all_values = lax.ppermute(
+                all_values,
+                device_axis,
+                tuple(((nth, (nth + 1) % seen_now) for nth in range(seen_now))),
+            )
+            front = lax.dynamic_update_slice_in_dim(
+                front, all_values, (x_next - w) % seen_now * new, axis=dim_at
+            )
+            if 2 * w < seen_now:
+                x_new = lax.ppermute(
+                    x_new,
+                    device_axis,
+                    tuple(((nth, (nth - 1) % seen_now) for nth in range(seen_now))),
+                )
+                front = lax.dynamic_update_slice_in_dim(
+                    front, x_new, (x_next + w) % seen_now * new, axis=dim_at
+                )
+        return front
+
     gathered = (
         lax.all_gather(qkv_weight, "fsdp", axis=0, tiled=True),
         lax.all_gather(proj_weight, "fsdp", axis=1, tiled=True),
         lax.all_gather(gelu_weight, "fsdp", axis=0, tiled=True),
-        lax.all_gather(down_weight, "fsdp", axis=1, tiled=True),
+        mark_the_body(down_weight, device_axis="fsdp", dim_at=1),
         lax.all_gather(attn_gain, "fsdp", axis=0, tiled=True),
         lax.all_gather(mlp_gain, "fsdp", axis=0, tiled=True),
     )

time: 700 us -> 700 us (level)
  blocking collectives: 44.7 us -> 27.9 us
  starting transfers between devices: 0.67 us -> 9.74 us
    all_gather x1 -> x0, blocking collectives: 16.8 us -> none  [on_device(): lax.all_gather(down_weight, 'fsdp', axis=1, tiled=True)]
    ppermute x0 -> x7, waiting for transfers between devices: none -> 11.5 us  [the longest x4 11.5 us: mark_the_body(): lax.ppermute(all_values, device_axis, tuple(((nth, (nth + 1) % seen_now)...]
    ppermute x0 -> x7, starting transfers between devices: none -> 8.89 us  [the longest x3 8.25 us: mark_the_body(): lax.ppermute(x_new, device_axis, tuple(((nth, (nth - 1) % seen_now) for n...]
  transfers between devices with their start and end apart: 11 -> 18, of which waited for: 11 -> 13; matrix products, arithmetic and copies ran while one was open for 7% -> 7% of each run, Pallas kernels for 0% -> 0%
where the time goes in v1:
time: 700 us; the launch traced here: 699 us
  waiting for transfers between devices  505 us (72%)
  local copies, waits for them, and re-layouts  56.1 us (8%)
  matrix products  54 us (8%)
  other arithmetic  30.3 us (4%)
  blocking collectives  27.9 us (4%)
  between operations  15.3 us (2%)
  starting transfers between devices  9.74 us (1%)
    psum x1, waiting for transfers between devices, on_device(): packed = lax.psum(packed, 'context')  94.9 us
    reduce_scatter x1, waiting for transfers between devices, on_device(): lax.psum_scatter(back_result[2].astype(jnp.bfloat16), 'context', scatter_...  74.8 us
    reduce_scatter x1, waiting for transfers between devices, on_device(): lax.psum_scatter(back_result[1].astype(jnp.bfloat16), 'context', scatter_...  67.6 us
    reduce_scatter x1, waiting for transfers between devices, on_device(): packed = lax.psum_scatter(packed, 'fsdp', scatter_dimension=0, tiled=True)  62.2 us
    all_gather x1, waiting for transfers between devices, on_device(): lax.all_gather(value_flat, 'context', axis=0, tiled=True)  42.2 us
    psum x1, waiting for transfers between devices, on_device(): lax.psum(jnp.dot(gate_up_grad, gelu_flat.T, preferred_element_type=jnp.fl...  41.8 us
    psum x1, waiting for transfers between devices, on_device(): residual = inputs + lax.psum(attn_part, 'tensor')  41.2 us
    psum x1, waiting for transfers between devices, on_device(): lax.psum(mlp_part.astype(jnp.bfloat16), 'tensor').astype(jnp.float32)  32.8 us
  transfers between devices with their start and end apart: 18, of which 13 were waited for; matrix products, arithmetic and copies ran while one was open for 7% of the time, Pallas kernels for 0%

profile of v1, /device:TPU:0, one launch (start us, length us, event | category | flops | bytes accessed | tf_op | source)
XLA Modules:
  0.0 698.9 jit_solution(6228193635920748750)
XLA Ops:
  11.6 14.7 %all-reduce.2 = (bf16[768]{0:T(1024)(128)(2,1)S(1)}, bf16[768]{0:T(1024)(128)(2,1)S(1)}) all-reduce(bf16[768]{0:T(1024)(128)(2,1)S(1)} %dynamic-update-slice, bf16[768]{0:T(1024)(128)(2,1)S(1)} %dynamic-update-slice.1), channel_id=1, replica_groups=mesh['fsdp'=8,'tensor'=2,'context'=8] {'fsdp'}, use_global_device_ids=true, to_apply=%add | all-reduce | flops 1536 | bytes 6144
  30.6 6.5 all-gather.5.cloned.1.call-done
  37.1 2.6 copy.52
  44.6 2.7 collective-permute-start.1
  48.6 13.2 %all_gather.27 = bf16[384,768]{0,1:T(8,128)(2,1)S(1)} all-gather(bf16[384,96]{0,1:T(8,128)(2,1)S(1)} %copy-done.47), channel_id=1, replica_groups=mesh['fsdp'=8,'tensor'=2,'context'=8] {'fsdp'}, dimensions={1}, use_global_device_ids=true | all-gather | bytes 663552 | tf_op jit(solution)/shard_map/all_gather | solution.py:156
  62.3 2.6 collective-permute-start.3
  64.9 27.8 %all-gather.9.cloned.1.call-done = bf16[2048,384]{0,1:T(8,128)(2,1)} async-done(((bf16[256,384]{0,1:T(8,128)(2,1)}), bf16[2048,384]{0,1:T(8,128)(2,1)}) %all-gather.9.cloned.1.call-update) | async-done | bytes 1572880 | tf_op jit(solution)/shard_map/all_gather | solution.py:181
  92.7 3.9 select_reduce_fusion.1
  96.6 3.9 select_reduce_fusion
  101.1 42.2 %all-gather.7.cloned.1.call-done = bf16[2048,384]{0,1:T(8,128)(2,1)} async-done(((bf16[256,384]{0,1:T(8,128)(2,1)}), bf16[2048,384]{0,1:T(8,128)(2,1)}) %all-gather.7.cloned.1.call-update) | async-done | bytes 1572880 | tf_op jit(solution)/shard_map/all_gather | solution.py:182
  143.3 7.6 %fusion.13 = bf16[6,64,256]{2,1,0:T(8,128)(2,1)S(1)} fusion(bf16[2048,6,64]{0,2,1:T(8,128)(2,1)} %bitcast.188, f32[6,256,2048]{2,1,0:T(8,128)} %copy-done.7, f32[6,256]{1,0:T(8,128)S(1)} %log_add_fusion, pred[256,2048]{1,0:T(8,128)(4,1)S(1)} %broadcast_compare_fusion.1), kind=kOutput, calls=%fused_computation.38 | convolution fusion | flops 415334400 | bytes 14882816 | tf_op jit(solution)/shard_map/hqk,khd->qhd/dot_general | solution.py:199
  152.6 2.9 collective-permute-start.5
  155.6 4.9 collective-permute-done.4
  160.5 6.6 collective-permute-done.6
  169.2 2.7 copy.54
  171.9 41.2 %all-reduce.9.cloned.1.call-done = f32[256,768]{1,0:T(8,128)} async-done(((f32[256,768]{1,0:T(8,128)}), f32[256,768]{1,0:T(8,128)}) %all-reduce.9.cloned.1.call-update) | async-done | bytes 786448 | tf_op jit(solution)/shard_map/psum | solution.py:204
  220.1 41.8 %all-reduce.11.cloned.1.call-done = f32[256,768]{1,0:T(8,128)} async-done(((f32[256,768]{1,0:T(8,128)}), f32[256,768]{1,0:T(8,128)}) %all-reduce.11.cloned.1.call-update) | async-done | bytes 786448 | tf_op jit(solution)/shard_map/psum | solution.py:228
  270.8 40.4 %while.20 = (s32[]{:T(128)}, f32[256,6,64]{0,2,1:T(8,128)}, f32[2048,384]{0,1:T(8,128)}, f32[2048,384]{0,1:T(8,128)}, bf16[2048,384]{0,1:T(8,128)(2,1)}, /*index...) while((s32[]{:T(128)}, f32[256,6,64]{0,2,1:T(8,128)}, ...), condition=%wide.region_19.20_spmd.clone, body=%wide.region_17.19_spmd.clone.sunk | while | flops 1024107520 | bytes 131182336 | solution.py:84
  275.3 3.3 fusion.105
  281.3 4.3 fusion.107
  295.5 3.3 fusion.105
  298.9 2.7 fusion.106
  301.5 4.3 fusion.107
  311.2 3.4 convert_element_type.160
  319.2 2.7 fusion.48
  321.9 67.6 %reduce-scatter.4.cloned.1.call-done = bf16[256,384]{0,1:T(8,128)(2,1)} async-done(((bf16[2048,384]{0,1:T(8,128)(2,1)}), bf16[256,384]{0,1:T(8,128)(2,1)}) %reduce-scatter.4.cloned.1.call-update) | async-done | bytes 196624 | tf_op jit(solution)/shard_map/reduce_scatter | solution.py:315
  391.4 74.8 %reduce-scatter.6.cloned.1.call-done = bf16[256,384]{0,1:T(8,128)(2,1)} async-done(((bf16[2048,384]{0,1:T(8,128)(2,1)}), bf16[256,384]{0,1:T(8,128)(2,1)}) %reduce-scatter.6.cloned.1.call-update) | async-done | bytes 196624 | tf_op jit(solution)/shard_map/reduce_scatter | solution.py:318
  469.6 3.0 convolution_bitcast_fusion
  476.8 32.8 %all-reduce.15.cloned.1.call-done = (bf16[256,768]{1,0:T(8,128)(2,1)}, bf16[256,768]{1,0:T(8,128)(2,1)}) async-done(((bf16[256,768]{1,0:T(8,128)(2,1)}, bf16[256,768]{1,0:T(8,128)(2,1)}), (bf16[256,768]{1,0:T(8,128)(2,1)}, bf16[256,768]{1,0:T(8,128)(2,1)})) %all-reduce.15.cloned.1.call-update) | async-done | bytes 786448 | tf_op jit(solution)/shard_map/psum | solution.py:216
  511.2 13.5 %concatenate.21 = f32[768,3266]{1,0:T(8,128)} concatenate(f32[768,1]{1,0:T(8,128)S(1)} %broadcast_in_dim.145, f32[768,1]{1,0:T(8,128)S(1)} %broadcast_in_dim.146, f32[768,1152]{1,0:T(8,128)} %fusion.45, f32[768,1152]{1,0:T(8,128)} %fusion.48, f32[768,384]{1,0:T(8,128)} %fusion.38, f32[768,576]{1,0:T(8,128)} %convolution_bitcast_fusion), dimensions={1} | concatenate | bytes 20066304 | tf_op jit(solution)/shard_map/concatenate | solution.py:354
  524.8 62.2 %reduce-scatter.8.cloned.1.call-done = f32[96,3266]{1,0:T(8,128)} async-done(((f32[768,3266]{1,0:T(8,128)}), f32[96,3266]{1,0:T(8,128)}) %reduce-scatter.8.cloned.1.call-update) | async-done | bytes 1254160 | tf_op jit(solution)/shard_map/reduce_scatter | solution.py:355
  589.0 94.9 %all-reduce.13.cloned.1.call-done = f32[96,3266]{1,0:T(8,128)} async-done(((f32[96,3266]{1,0:T(8,128)}), f32[96,3266]{1,0:T(8,128)}) %all-reduce.13.cloned.1.call-update) | async-done | bytes 1254160 | tf_op jit(solution)/shard_map/psum | solution.py:356
  (288 shorter events, 82.7 us)
Async XLA Ops:
  7.2 29.9 %all-gather.5.cloned.1.call-start = ((), (), s32[]{:S(2)}) async-start(), calls=%async_computation.3 | async-start | bytes 1990656 | tf_op jit(solution)/shard_map/all_gather | solution.py:155
  7.9 84.8 %all-gather.9.cloned.1.call-start = ((), (), s32[]{:S(2)}) async-start(), calls=%async_computation.5 | async-start | bytes 1769472 | tf_op jit(solution)/shard_map/all_gather | solution.py:181
  41.8 54.8 %copy-start.34 = (bf16[256,6,32]{0,2,1:T(8,128)(2,1)}, bf16[256,6,32]{0,2,1:T(8,128)(2,1)S(1)}, u32[]{:S(2)}) copy-start(bf16[256,6,32]{0,2,1:T(8,128)(2,1)S(1)} %get-tuple-element.409) | copy-start | bytes 294916
  41.8 54.8 %copy-start.36 = (bf16[256,6,32]{0,2,1:T(8,128)(2,1)}, bf16[256,6,32]{0,2,1:T(8,128)(2,1)S(1)}, u32[]{:S(2)}) copy-start(bf16[256,6,32]{0,2,1:T(8,128)(2,1)S(1)} %get-tuple-element.410) | copy-start | bytes 294916
  42.5 100.8 %all-gather.7.cloned.1.call-start = ((), (), s32[]{:S(2)}) async-start(), calls=%async_computation.4 | async-start | bytes 1769472 | tf_op jit(solution)/shard_map/all_gather | solution.py:182
  44.3 124.9 %all-gather.11.cloned.1.call-start = ((), (), s32[]{:S(2)}) async-start(), calls=%async_computation.7 | async-start | bytes 2211840 | tf_op jit(solution)/shard_map/all_gather | solution.py:157
  44.4 17.6 %collective-permute-start = (bf16[576,96]{0,1:T(8,128)(2,1)S(1)}, bf16[576,96]{0,1:T(8,128)(2,1)S(1)}, u32[]{:S(2)}, u32[]{:S(2)}) collective-permute-start(bf16[576,96]{0,1:T(8,128)(2,1)S(1)} %copy-done.46), channel_id=1, source_target_pairs={{0,16},{16,32},{32,48},{48,64},{64,80},{80,96},{96,112},{112,0},{1... | collective-permute-start | bytes 331784 | tf_op jit(solution)/shard_map/ppermute | solution.py:135
  44.6 17.7 %collective-permute-start.1 = (bf16[576,96]{0,1:T(8,128)(2,1)S(1)}, bf16[576,96]{0,1:T(8,128)(2,1)S(1)}, u32[]{:S(2)}, u32[]{:S(2)}) collective-permute-start(bf16[576,96]{0,1:T(8,128)(2,1)S(1)} %copy-done.46), channel_id=1, source_target_pairs={{0,112},{16,0},{32,16},{48,32},{64,48},{80,64},{96,80},{112,96},{1... | collective-permute-start | bytes 331784 | tf_op jit(solution)/shard_map/ppermute | solution.py:144
  48.1 165.0 %all-reduce.9.cloned.1.call-start = ((), (), s32[]{:S(2)}) async-start(), calls=%async_computation.6 | async-start | bytes 1572864 | tf_op jit(solution)/shard_map/psum | solution.py:204
  61.8 89.1 %copy-start.19 = (bf16[384,768]{0,1:T(8,128)(2,1)}, bf16[384,768]{0,1:T(8,128)(2,1)S(1)}, u32[]{:S(2)}) copy-start(bf16[384,768]{0,1:T(8,128)(2,1)S(1)} %all_gather.27) | copy-start | bytes 1769476
  61.9 90.6 %collective-permute-start.2 = (bf16[576,96]{0,1:T(8,128)(2,1)S(1)}, bf16[576,96]{0,1:T(8,128)(2,1)S(1)}, u32[]{:S(2)}, u32[]{:S(2)}) collective-permute-start(bf16[576,96]{0,1:T(8,128)(2,1)S(1)} %collective-permute-done), channel_id=1, source_target_pairs={{0,16},{16,32},{32,48},{48,64},{64,80},{80,96},{96,112},{112,0},{1... | collective-permute-start | bytes 331784 | tf_op jit(solution)/shard_map/ppermute | solution.py:135
  62.3 90.3 %collective-permute-start.3 = (bf16[576,96]{0,1:T(8,128)(2,1)S(1)}, bf16[576,96]{0,1:T(8,128)(2,1)S(1)}, u32[]{:S(2)}, u32[]{:S(2)}) collective-permute-start(bf16[576,96]{0,1:T(8,128)(2,1)S(1)} %collective-permute-done.1), channel_id=1, source_target_pairs={{0,112},{16,0},{32,16},{48,32},{64,48},{80,64},{96,80},{112,96},{1... | collective-permute-start | bytes 331784 | tf_op jit(solution)/shard_map/ppermute | solution.py:144
  101.1 49.8 %copy-start.59 = (f32[6,256]{1,0:T(8,128)}, f32[6,256]{1,0:T(8,128)S(1)}, u32[]{:S(2)}) copy-start(f32[6,256]{1,0:T(8,128)S(1)} %log_add_fusion) | copy-start | bytes 18436
  152.2 109.6 %all-reduce.11.cloned.1.call-start = ((), (), s32[]{:S(2)}) async-start(), calls=%async_computation.8 | async-start | bytes 1572864 | tf_op jit(solution)/shard_map/psum | solution.py:228
  152.5 7.9 %collective-permute-start.4 = (bf16[576,96]{0,1:T(8,128)(2,1)S(1)}, bf16[576,96]{0,1:T(8,128)(2,1)S(1)}, u32[]{:S(2)}, u32[]{:S(2)}) collective-permute-start(bf16[576,96]{0,1:T(8,128)(2,1)S(1)} %collective-permute-done.2), channel_id=1, source_target_pairs={{0,16},{16,32},{32,48},{48,64},{64,80},{80,96},{96,112},{112,0},{1... | collective-permute-start | bytes 331784 | tf_op jit(solution)/shard_map/ppermute | solution.py:135
  152.6 7.9 %collective-permute-start.5 = (bf16[576,96]{0,1:T(8,128)(2,1)S(1)}, bf16[576,96]{0,1:T(8,128)(2,1)S(1)}, u32[]{:S(2)}, u32[]{:S(2)}) collective-permute-start(bf16[576,96]{0,1:T(8,128)(2,1)S(1)} %collective-permute-done.3), channel_id=1, source_target_pairs={{0,112},{16,0},{32,16},{48,32},{64,48},{80,64},{96,80},{112,96},{1... | collective-permute-start | bytes 331784 | tf_op jit(solution)/shard_map/ppermute | solution.py:144
  160.5 6.6 collective-permute-start.6
  171.9 45.6 %copy-start.32 = (bf16[256,768]{1,0:T(8,128)(2,1)S(1)}, bf16[256,768]{1,0:T(8,128)(2,1)}, u32[]{:S(2)}) copy-start(bf16[256,768]{1,0:T(8,128)(2,1)} %param.19) | copy-start | bytes 1179652
  214.5 49.5 %copy-start.8 = (f32[256,768]{1,0:T(8,128)}, f32[256,768]{1,0:T(8,128)S(1)}, u32[]{:S(2)}) copy-start(f32[256,768]{1,0:T(8,128)S(1)} %get-tuple-element.396) | copy-start | bytes 2359300
  218.0 46.0 %copy-start.43 = (bf16[256,1,576]{0,2,1:T(8,128)(2,1)}, bf16[256,1,576]{0,2,1:T(8,128)(2,1)S(1)}, u32[]{:S(2)}) copy-start(bf16[256,1,576]{0,2,1:T(8,128)(2,1)S(1)} %get-tuple-element.399) | copy-start | bytes 884740
  218.0 45.9 %copy-start.44 = (bf16[256,1,576]{0,2,1:T(8,128)(2,1)}, bf16[256,1,576]{0,2,1:T(8,128)(2,1)S(1)}, u32[]{:S(2)}) copy-start(bf16[256,1,576]{0,2,1:T(8,128)(2,1)S(1)} %get-tuple-element.400) | copy-start | bytes 884740
  218.1 45.9 %copy-start.33 = (bf16[256,768]{1,0:T(8,128)(2,1)S(1)}, bf16[256,768]{1,0:T(8,128)(2,1)}, u32[]{:S(2)}) copy-start(bf16[256,768]{1,0:T(8,128)(2,1)} %param.19) | copy-start | bytes 1179652
  219.8 45.7 %copy-start.20 = (bf16[384,768]{0,1:T(8,128)(2,1)S(1)}, bf16[384,768]{0,1:T(8,128)(2,1)}, u32[]{:S(2)}) copy-start(bf16[384,768]{0,1:T(8,128)(2,1)} %copy-done.19) | copy-start | bytes 1769476
  219.8 169.7 %reduce-scatter.4.cloned.1.call-start = ((), (), s32[]{:S(2)}) async-start(), calls=%async_computation.9 | async-start | bytes 1769472 | tf_op jit(solution)/shard_map/reduce_scatter | solution.py:315
  314.7 151.5 %reduce-scatter.6.cloned.1.call-start = ((), (), s32[]{:S(2)}) async-start(), calls=%async_computation.10 | async-start | bytes 1769472 | tf_op jit(solution)/shard_map/reduce_scatter | solution.py:318
  316.2 193.4 %all-reduce.15.cloned.1.call-start = ((), (), s32[]{:S(2)}) async-start(), calls=%async_computation.13 | async-start | bytes 1572864 | tf_op jit(solution)/shard_map/psum | solution.py:216
  319.2 71.3 %copy-start.14 = (f32[256,6,64]{0,2,1:T(8,128)S(1)}, f32[256,6,64]{0,2,1:T(8,128)}, u32[]{:S(2)}) copy-start(f32[256,6,64]{0,2,1:T(8,128)} %get-tuple-element.285) | copy-start | bytes 1179652
  319.2 148.8 %copy-start.13 = (bf16[768,3,384]{0,2,1:T(8,128)(2,1)S(1)}, bf16[768,3,384]{0,2,1:T(8,128)(2,1)}, u32[]{:S(2)}) copy-start(bf16[768,3,384]{0,2,1:T(8,128)(2,1)} %copy-done.12) | copy-start | bytes 5308420
  469.5 117.5 %reduce-scatter.8.cloned.1.call-start = ((), (), s32[]{:S(2)}) async-start(), calls=%async_computation.11 | async-start | bytes 11501568 | tf_op jit(solution)/shard_map/reduce_scatter | solution.py:355
  524.7 62.3 %copy-start.40 = (bf16[256,768]{1,0:T(8,128)(2,1)S(1)}, bf16[256,768]{1,0:T(8,128)(2,1)}, u32[]{:S(2)}) copy-start(bf16[256,768]{1,0:T(8,128)(2,1)} %get-tuple-element.393) | copy-start | bytes 1179652
  524.7 63.2 %copy-start.31 = (bf16[256,768]{1,0:T(8,128)(2,1)S(1)}, bf16[256,768]{1,0:T(8,128)(2,1)}, u32[]{:S(2)}) copy-start(bf16[256,768]{1,0:T(8,128)(2,1)} %get-tuple-element.394) | copy-start | bytes 1179652
  524.7 159.2 %all-reduce.13.cloned.1.call-start = ((), (), s32[]{:S(2)}) async-start(), calls=%async_computation.12 | async-start | bytes 2555904 | tf_op jit(solution)/shard_map/psum | solution.py:356
  (65 other events, 338.5 us)
Sparse Core Ops, SparseCore 0:
  9.7 27.3 all-gather.4
  42.7 50.0 all-gather.8
  95.5 47.7 all-gather.6
  145.4 23.7 all-gather.10
  172.1 40.9 all-reduce.8
  219.9 41.9 all-reduce.10
  314.8 74.6 reduce-scatter.3
  393.7 72.4 reduce-scatter.5
  469.6 39.9 all-reduce.14
  524.9 62.0 reduce-scatter.7
  589.7 94.2 all-reduce.12
